TPU v7x, 32 devices: a whole 2x2x4 slice. The times are simulated.
32 devices in a mesh: grp: 8 (over z, y), rep: 2 (over core), tp: 2 (over x).
Axes of the slice: x: 2, y: 2, z: 4, core: 2. Of those that a mesh axis runs over, the one named last changes fastest.
Arguments:
- hidden: bfloat16 [8, 768, 8192], P('grp', 'rep'), may hold values from -6 to 6
- decode_hidden: bfloat16 [8, 2, 2, 32, 8192], P('grp', 'rep'), may hold values from -6 to 6
- norm_gain: bfloat16 [8192], replicated, may hold values from 0.25 to 1.75
- qkv_weight: bfloat16 [8192, 10240], P('grp', 'tp'), may hold values from -0.0625 to 0.0625
- qkv_bias: bfloat16 [10240], P('tp'), may hold values from -32 to 32
- lengths: int32 [8], replicated, may hold values from 12 to 768, as said below
Outputs:
- prefill_out: bfloat16 [8, 768, 8192], P('grp', 'rep', 'tp')
- decode_out: bfloat16 [8, 2, 2, 32, 8192], P('grp', 'rep', None, None, 'tp')
Inputs may be any that keep to these rules, and one draw needn't show every extreme that they name: `lengths`: some prompt is 768 tokens long.
All inputs are finite; a program needn't handle non-finite values.
Results may differ from a plain program's by a relative error of at most 0.012.
The roundings to bfloat16 on the way count: a program that leaves them out, or rounds other values in their place, can miss the bound.
Values may be sent and summed in bfloat16 or wider, within the bound.
A program may use at most 256 MiB of HBM per device.

v0:
```python
import jax
import jax.numpy as jnp
from jax import lax
from jax.sharding import PartitionSpec as P

HD = 128
QPK = 8
STEPS = 4


THETA = 1000000.0
EPSILON = 1e-06
NEGATIVE = -1e30


def shifted(block, axis, distance):
    devices = range(lax.axis_size(axis))
    route = [((i - distance) % len(devices), i) for i in devices]
    return lax.ppermute(block, axis, route)


def normalize(row_block, gain_row):
    widened = row_block.astype(jnp.float32)
    factor = lax.rsqrt(jnp.mean(widened * widened, axis=-1, keepdims=True) + EPSILON)
    return (widened * factor * gain_row.astype(jnp.float32)).astype(jnp.bfloat16)


def rope_tables(positions, head_size):
    half_size = head_size // 2
    frequency = THETA ** (-(jnp.arange(half_size, dtype=jnp.float32) * 2.0 / head_size))
    angle = positions.astype(jnp.float32)[:, None] * frequency[None, :]
    return (jnp.cos(angle), jnp.sin(angle))


def rotate(vector, cosine, sine_part):
    half_size = vector.shape[-1] // 2
    first_half = vector[..., :half_size]
    second = vector[..., half_size:]
    return jnp.concatenate(
        [first_half * cosine - second * sine_part, second * cosine + first_half * sine_part],
        axis=-1,
    )


def masked_max(scores, allowed):
    return jnp.max(jnp.where(allowed, scores, NEGATIVE), axis=-1, keepdims=True)


def combine_values(weight_matrix, value_matrix):
    return jnp.einsum(
        "aprk,kaz->rapz",
        weight_matrix.astype(jnp.bfloat16),
        value_matrix,
        preferred_element_type=jnp.float32,
    )


def pair_scores(query_matrix, key_matrix_rows, score_scale):
    return (
        jnp.einsum(
            "wjro,ujo->jrwu", query_matrix, key_matrix_rows, preferred_element_type=jnp.float32
        )
        * score_scale
    )


def decode_pair(
    query_matrix,
    own_keys,
    own_values,
    prompt_keys,
    prompt_values,
    valid_len,
    local_allowed,
    score_scale,
):
    key_slot_index = jnp.arange(prompt_keys.shape[0], dtype=jnp.int32)
    prompt_allowed = (key_slot_index < valid_len)[None, None, None, :]
    far_scores = pair_scores(query_matrix, prompt_keys, score_scale)
    near_scores = pair_scores(query_matrix, own_keys, score_scale)
    highest = jnp.maximum(
        masked_max(far_scores, prompt_allowed), masked_max(near_scores, local_allowed)
    )
    far_exp = jnp.where(prompt_allowed, jnp.exp(far_scores - highest), 0.0)
    near_exp = jnp.where(local_allowed, jnp.exp(near_scores - highest), 0.0)
    running = jnp.sum(far_exp, axis=-1, keepdims=True) + jnp.sum(near_exp, axis=-1, keepdims=True)
    return combine_values(far_exp / running, prompt_values) + combine_values(
        near_exp / running, own_values
    )


def on_device(hidden, decode_hidden, norm_gain, qkv_weight, qkv_bias, lengths):
    prompt_count = lax.axis_size("grp")
    rep_count = lax.axis_size("rep")
    half_cycle = prompt_count // 2
    grp_here = lax.axis_index("grp")
    rep_here = lax.axis_index("rep")
    span_rows = hidden.shape[1]
    model_width = hidden.shape[2]
    head_block = (QPK + 2) * HD
    heads_here = qkv_bias.shape[0] // head_block
    decode_rows = decode_hidden.shape[3]
    score_scale = HD ** (-0.5)
    prefill_normed = normalize(hidden[0], norm_gain)
    decode_normed = normalize(decode_hidden.reshape(2 * decode_rows, model_width), norm_gain)
    normed = jnp.concatenate([prefill_normed, decode_normed], axis=0)
    share_cols = qkv_weight.shape[1] // rep_count
    own_cols = lax.dynamic_slice_in_dim(qkv_weight, rep_here * share_cols, share_cols, 1)
    columns = lax.all_gather(own_cols, "grp", axis=0, tiled=True)
    complete = lax.all_gather(columns, "rep", axis=1, tiled=True)
    projected = jnp.dot(normed, complete, preferred_element_type=jnp.float32)
    projected = (projected + qkv_bias.astype(jnp.float32)).reshape(
        normed.shape[0], heads_here, QPK + 2, HD
    )
    index_table = jnp.arange(prompt_count, dtype=jnp.int32)

    def length_of(prompt):
        return jnp.sum(jnp.where(index_table == prompt, lengths, 0))

    own_len = length_of(grp_here)
    far_len = length_of((grp_here + half_cycle) % prompt_count)
    row_position = rep_here * span_rows + jnp.arange(span_rows, dtype=jnp.int32)
    local_ids = jnp.arange(decode_rows, dtype=jnp.int32)
    step_ids = local_ids % STEPS
    sample_ids = local_ids // STEPS
    positions = jnp.concatenate([row_position, own_len + step_ids, far_len + step_ids])
    cosine, sine_part = rope_tables(positions, HD)
    query_matrix = rotate(
        projected[:, :, :QPK], cosine[:, None, None, :], sine_part[:, None, None, :]
    ).astype(jnp.bfloat16)
    key_matrix_rows = rotate(
        projected[:, :, QPK], cosine[:, None, :], sine_part[:, None, :]
    ).astype(jnp.bfloat16)
    value_matrix = projected[:, :, QPK + 1].astype(jnp.bfloat16)
    cache_keys, cache_values = (
        lax.all_gather(key_matrix_rows[:span_rows], "rep", axis=0, tiled=True),
        lax.all_gather(value_matrix[:span_rows], "rep", axis=0, tiled=True),
    )
    key_pos = jnp.arange(cache_keys.shape[0], dtype=jnp.int32)
    allowed = ((key_pos[None, :] <= row_position[:, None]) & (key_pos[None, :] < own_len))[
        None, None
    ]
    scores = pair_scores(query_matrix[:span_rows], cache_keys, score_scale)
    highest = masked_max(scores, allowed)
    exponent = jnp.where(allowed, jnp.exp(scores - highest), 0.0)
    weight_matrix = exponent / jnp.sum(exponent, axis=-1, keepdims=True)
    attended = combine_values(weight_matrix, cache_values)
    prefill_out = attended.astype(jnp.bfloat16).reshape(1, span_rows, heads_here * QPK * HD)
    decode_queries = query_matrix[span_rows:].reshape(2, decode_rows, heads_here, QPK, HD)
    decode_keys = key_matrix_rows[span_rows:].reshape(2, decode_rows, heads_here, HD)
    decode_values = value_matrix[span_rows:].reshape(2, decode_rows, heads_here, HD)
    local_allowed = (
        (sample_ids[None, :] == sample_ids[:, None]) & (step_ids[None, :] <= step_ids[:, None])
    )[None, None]
    near_out = decode_pair(
        decode_queries[0],
        decode_keys[0],
        decode_values[0],
        cache_keys,
        cache_values,
        own_len,
        local_allowed,
        score_scale,
    )
    far_keys, far_values = shifted((cache_keys, cache_values), "grp", half_cycle)
    far_out = decode_pair(
        decode_queries[1],
        decode_keys[1],
        decode_values[1],
        far_keys,
        far_values,
        far_len,
        local_allowed,
        score_scale,
    )
    decode_out = (
        jnp.stack([near_out, far_out])
        .astype(jnp.bfloat16)
        .reshape(1, 1, 2, decode_rows, heads_here * QPK * HD)
    )
    return (prefill_out, decode_out)


def solution(mesh):
    return jax.shard_map(
        on_device,
        mesh=mesh,
        in_specs=(
            P("grp", "rep", None),
            P("grp", "rep", None, None, None),
            P(),
            P("grp", "tp"),
            P("tp"),
            P(),
        ),
        out_specs=(P("grp", "rep", "tp"), P("grp", "rep", None, None, "tp")),
        check_vma=False,
    )
```

profile of v0, /device:TPU:0, one launch (start us, length us, event | category | flops | bytes accessed | tf_op | source)
XLA Modules:
  0.0 1132.9 jit_solution(10912499802913706107)
XLA Ops:
  7.2 0.0 all-gather.4.cloned.1.call-start
  7.2 5.1 constant_dynamic-slice_fusion
  12.4 0.0 all-gather.4.cloned.1.call-update
  12.4 0.0 all-gather.6.cloned.1.call-start
  12.4 797.8 %all-gather.4.cloned.1.call-done = bf16[8192,2560]{1,0:T(8,128)(2,1)} async-done(((bf16[1024,2560]{1,0:T(8,128)(2,1)}), bf16[8192,2560]{1,0:T(8,128)(2,1)}) %all-gather.4.cloned.1.call-update) | async-done | bytes 41943056 | tf_op jit(solution)/shard_map/all_gather | solution.py:109
  810.2 0.0 all-gather.6.cloned.1.call-update
  810.3 0.7 copy-done.10
  810.9 0.5 copy-done.7
  811.5 0.3 multiply_reduce_fusion
  811.8 0.1 rsqrt.21
  811.9 0.6 fusion.74
  812.6 0.6 iota_compare_fusion.2
  813.2 1.3 broadcast_add_fusion
  814.5 1.2 iota_compare_fusion.1
  815.7 0.1 add_convert_fusion.2
  815.8 4.9 fusion.9
  820.8 0.7 compare_and_fusion
  821.4 0.9 fusion.40
  822.4 0.9 multiply_cosine_fusion
  823.3 0.3 fusion.32
  823.6 12.1 %fusion.11 = bf16[384,8192]{1,0:T(8,128)(2,1)} fusion(bf16[1,384,8192]{2,1,0:T(8,128)(2,1)} %param.6, f32[8192]{0:T(1024)S(1)} %convert_element_type.70, f32[384]{0:T(512)S(1)} %add_rsqrt_fusion), kind=kLoop, calls=%fused_computation.16 | loop fusion | flops 12582912 | bytes 12617216 | tf_op jit(solution)/shard_map/convert_element_type | solution.py:25
  835.6 95.3 %all-gather.6.cloned.1.call-done = bf16[8192,5120]{1,0:T(8,128)(2,1)} async-done(((bf16[8192,2560]{1,0:T(8,128)(2,1)}), bf16[8192,5120]{1,0:T(8,128)(2,1)}) %all-gather.6.cloned.1.call-update) | async-done | bytes 83886096 | tf_op jit(solution)/shard_map/all_gather | solution.py:110
  931.0 47.5 %fusion.16 = f32[448,5120]{1,0:T(8,128)} fusion(bf16[8192,5120]{1,0:T(8,128)(2,1)} %all-gather.6.cloned.1.call-done, bf16[64,8192]{1,0:T(8,128)(2,1)S(1)} %fusion.32, bf16[384,8192]{1,0:T(8,128)(2,1)} %fusion.11, f32[5120]{0:T(1024)S(1)} %convert_element_type.76), kind=kOutput, calls=%fused_computation.24 | convolution fusion | flops 37597937664 | bytes 100421632 | tf_op jit(solution)/shard_map/dot_general | solution.py:111
  978.5 10.8 copy.20
  989.3 1.3 slice.92
  990.6 8.8 fusion.92
  999.4 3.1 copy.59
  1002.5 0.3 copy.55
  1002.8 0.4 add_convert_fusion.1
  1003.2 0.0 copy-start.3
  1003.2 0.7 copy-done.3
  1004.0 0.2 fusion.59
  1004.2 2.5 all_gather.15
  1006.7 6.5 copy.56
  1013.2 6.5 copy.57
  1019.7 6.3 add_convert_fusion
  1026.1 0.1 pad_maximum_fusion.1
  1026.3 1.6 copy-done.1
  1027.9 1.1 copy-done.2
  1029.0 1.9 fusion.25
  1030.9 2.7 collective-permute-start.1
  1033.6 26.4 %fusion.93 = (f32[4,8,384]{2,1,0:T(8,128)S(1)}, f32[4,8,384,768]{2,3,1,0:T(8,128)}) fusion(pred[384,768]{0,1:T(8,128)(4,1)} %fusion.40, bf16[768,4,128]{2,0,1:T(8,128)(2,1)} %all_gather.15, bf16[448,4,8,64]{3,0,2,1:T(8,128)(2,1)} %copy-done.2, bf16[448,4,8,64]{3,0,2,1:T(8,128)(2,1)} %copy-done.1), kind=kOutput, calls=%fused_computation.139 | convolution fusion | flops 4901044736 | bytes 54640640 | tf_op jit(solution)/shard_map/sub | solution.py:145
  1060.0 1.0 slice.91
  1061.1 2.5 all-gather
  1063.6 15.2 %fusion.30 = bf16[4,128,8,384]{3,1,2,0:T(8,128)(2,1)} fusion(f32[4,8,384,768]{2,3,1,0:T(8,128)} %get-tuple-element.19, f32[4,8,384]{2,1,0:T(8,128)S(1)} %get-tuple-element.18, bf16[768,4,1,128]{0,3,1,2:T(8,128)(2,1)} %all-gather), kind=kOutput, calls=%fused_computation.45 | convolution fusion | flops 2436366336 | bytes 41730048 | tf_op jit(solution)/shard_map/aprk,kaz->rapz/dot_general | solution.py:50
  1078.8 4.6 copy.34
  1083.5 1.8 select_reduce_fusion.1
  1085.2 0.3 collective-permute-start
  1085.6 0.8 fusion.28
  1086.4 1.4 fusion.57
  1087.8 2.1 fusion.33
  1089.9 0.0 copy-start.8
  1089.9 1.3 fusion.41
  1091.2 0.1 copy.29
  1091.3 0.1 stack.9
  1091.4 1.8 fusion.22
  1093.2 0.1 fusion.58
  1093.4 0.8 fusion.29
  1094.2 1.3 fusion.64
  1095.5 27.3 %collective-permute-done = bf16[768,4,128]{0,2,1:T(8,128)(2,1)} collective-permute-done((bf16[768,4,128]{0,2,1:T(8,128)(2,1)}, bf16[768,4,128]{0,2,1:T(8,128)(2,1)}, u32[]{:S(2)}, u32[]{:S(2)}) %collective-permute-start) | collective-permute-done | bytes 786464 | tf_op jit(solution)/shard_map/ppermute | solution.py:19
  1122.9 2.2 fusion.42
  1125.0 0.1 copy.33
  1125.1 0.1 stack.10
  1125.3 0.8 pad_maximum_fusion
  (33 shorter events, 0.1 us)
Async XLA Ops:
  7.2 803.1 %all-gather.4.cloned.1.call-start = ((), (), s32[]{:S(2)}) async-start(), calls=%async_computation | async-start | bytes 47185920 | tf_op jit(solution)/shard_map/all_gather | solution.py:109
  12.4 918.6 %all-gather.6.cloned.1.call-start = ((), (), s32[]{:S(2)}) async-start(), calls=%async_computation.1 | async-start | bytes 125829120 | tf_op jit(solution)/shard_map/all_gather | solution.py:110
  810.2 0.7 copy-start.10
  810.2 1.2 copy-start.7
  810.2 1.6 copy-start.11
  810.2 1.7 copy-start.13
  990.6 8.8 copy-start
  1003.2 0.8 copy-start.3
  1003.2 1.0 copy-start.5
  1026.1 1.8 copy-start.1
  1026.1 2.9 copy-start.2
  1030.9 60.5 %collective-permute-start.1 = (bf16[768,4,128]{2,0,1:T(8,128)(2,1)}, bf16[768,4,128]{2,0,1:T(8,128)(2,1)}, u32[]{:S(2)}, u32[]{:S(2)}) collective-permute-start(bf16[768,4,128]{2,0,1:T(8,128)(2,1)} %all_gather.15), channel_id=1, source_target_pairs={{16,0},{20,4},{24,8},{28,12},{0,16},{4,20},{8,24},{12,28},{17,1},{... | collective-permute-start | bytes 2359304 | tf_op jit(solution)/shard_map/ppermute | solution.py:19
  1078.8 4.6 copy-start.9
  1083.5 2.9 copy-start.4
  1083.5 2.9 copy-start.6
  1085.2 37.6 %collective-permute-start = (bf16[768,4,128]{0,2,1:T(8,128)(2,1)}, bf16[768,4,128]{0,2,1:T(8,128)(2,1)}, u32[]{:S(2)}, u32[]{:S(2)}) collective-permute-start(bf16[768,4,128]{0,2,1:T(8,128)(2,1)} %bitcast.4), channel_id=1, source_target_pairs={{16,0},{20,4},{24,8},{28,12},{0,16},{4,20},{8,24},{12,28},{17,1},{... | collective-permute-start | bytes 2359304 | tf_op jit(solution)/shard_map/ppermute | solution.py:19
  1087.8 3.6 copy-start.12
  1089.9 3.4 copy-start.8
Sparse Core Ops, SparseCore 0:
  12.5 797.6 all-gather.3
  811.8 119.1 all-gather.5
where the time goes:
time: 1130 us
  waiting for transfers between devices  921 us (82%)
  matrix products  103 us (9%)
  local copies, waits for them, and re-layouts  53.4 us (5%)
  other arithmetic  33.8 us (3%)
  between operations  14.4 us (1%)
    all_gather x1, waiting for transfers between devices, on_device(): columns = lax.all_gather(own_cols, 'grp', axis=0, tiled=True)  798 us
    all_gather x1, waiting for transfers between devices, on_device(): complete = lax.all_gather(columns, 'rep', axis=1, tiled=True)  95.3 us
    dot_general x1, matrix products, on_device(): projected = jnp.dot(normed, complete, preferred_element_type=jnp.float32)  47.5 us
    ppermute x2, waiting for transfers between devices, shifted(): return lax.ppermute(block, axis, route)  27.4 us
    sub x1, matrix products, on_device(): exponent = jnp.where(allowed, jnp.exp(scores - highest), 0.0)  26.4 us
    unnamed x32, local copies, waits for them, and re-layouts  22.7 us
  transfers between devices with their start and end apart: 4, of which 3 were waited for; matrix products, arithmetic and copies ran while one was open for 7% of the time, Pallas kernels for 0%

commit v1 on v0

--- a/solution.py
+++ b/solution.py
@@ -1,7 +1,11 @@
 import jax
 import jax.numpy as jnp
 from jax import lax
+from jax.experimental import pallas as pl
+from jax.experimental.pallas import tpu as pltpu
 from jax.sharding import PartitionSpec as P
+import functools
+import math
 
 HD = 128
 QPK = 8
@@ -89,7 +93,7 @@
     )
 
 
-def on_device(hidden, decode_hidden, norm_gain, qkv_weight, qkv_bias, lengths):
+def plain_device(hidden, decode_hidden, norm_gain, qkv_weight, qkv_bias, lengths):
     prompt_count = lax.axis_size("grp")
     rep_count = lax.axis_size("rep")
     half_cycle = prompt_count // 2
@@ -181,6 +185,429 @@
     return (prefill_out, decode_out)
 
 
+TILE = 512
+MESH = pl.DeviceIdType.MESH
+
+
+def gather_kernel(
+    size, rows_up, hidden_ref, decode_ref, gain_ref, w_ref,
+    acc_ref, wa_ref, wb_ref,
+    x_ref, wt_ref, sa, ra, sb, rb, sx, rx, lx, lt,
+):
+    count = size
+    depth = count // 2
+    g = lax.axis_index("grp")
+    r = lax.axis_index("rep")
+    z = g // 2
+    y = g % 2
+    half = count // 2
+    far = (g + half) % count
+    span = hidden_ref.shape[1]
+    drows = decode_ref.shape[3]
+    share = w_ref.shape[0]
+    cols_a = wa_ref.shape[2]
+    cols_b = wb_ref.shape[2]
+    tiles_a = cols_a // TILE
+    tiles_b = cols_b // TILE
+    base = pl.multiple_of(r * (cols_a + cols_b), 128)
+    base_b = pl.multiple_of(r * (cols_a + cols_b) + cols_a, 128)
+
+    barrier = pltpu.get_barrier_semaphore()
+
+    def greet(grp, rep):
+        pl.semaphore_signal(barrier, inc=1, device_id={"grp": grp, "rep": rep}, device_id_type=MESH)
+
+    greet(z * 2 + 1 - y, r)
+    greet(g, 1 - r)
+    greet(far, r)
+
+    @pl.when(z >= 1)
+    def _():
+        greet(g - 2, r)
+
+    @pl.when(z + 1 < depth)
+    def _():
+        greet(g + 2, r)
+
+    inner = (z >= 1) & (z + 1 < depth)
+
+    @pl.when(inner)
+    def _():
+        pl.semaphore_wait(barrier, 5)
+
+    @pl.when(jnp.logical_not(inner))
+    def _():
+        pl.semaphore_wait(barrier, 4)
+
+    def way(direction):
+        return (g - 2, g + 2, z * 2 + 1 - y)[direction]
+
+    def copy_a(o, direction, own):
+        src = w_ref.at[:, pl.ds(base, cols_a)] if own else wa_ref.at[o]
+        return pltpu.make_async_remote_copy(
+            src, wa_ref.at[o], sa.at[o, direction], ra.at[o],
+            device_id={"grp": way(direction)}, device_id_type=MESH,
+        )
+
+    def copy_b(o, direction, own):
+        src = w_ref.at[:, pl.ds(base_b, cols_b)] if own else wb_ref.at[o]
+        return pltpu.make_async_remote_copy(
+            src, wb_ref.at[o], sb.at[o, direction], rb.at[o],
+            device_id={"grp": way(direction)}, device_id_type=MESH,
+        )
+
+    def along(make, o, own, left, right):
+        @pl.when(left)
+        def _():
+            make(o, 0, own).start()
+
+        @pl.when(right)
+        def _():
+            make(o, 1, own).start()
+
+    row_h = pl.multiple_of(r * span, 16)
+    row_n = pl.multiple_of(2 * span + r * drows, 16)
+    row_f = pl.multiple_of(2 * span + (2 + r) * drows, 16)
+    row_o = pl.multiple_of(2 * span + (3 - r) * drows, 16)
+    sib = {"rep": 1 - r}
+
+    def send(src, row, n, i, device):
+        return pltpu.make_async_remote_copy(
+            src, x_ref.at[pl.ds(row, n), :], sx.at[i], rx.at[i], device_id=device, device_id_type=MESH
+        )
+
+    far_send = send(decode_ref.at[0, 0, 1], row_f, drows, 0, {"grp": far})
+    far_send.start()
+    along(copy_a, g, True, z >= 1, z + 1 < depth)
+    copy_b(g, 2, True).start()
+    copy_a(g, 2, True).start()
+    hid_send = send(hidden_ref.at[0], row_h, span, 1, sib)
+    near_send = send(decode_ref.at[0, 0, 0], row_n, drows, 2, sib)
+    hid_send.start()
+    near_send.start()
+    own_h = pltpu.make_async_copy(hidden_ref.at[0], x_ref.at[pl.ds(row_h, span), :], lx.at[0])
+    own_n = pltpu.make_async_copy(decode_ref.at[0, 0, 0], x_ref.at[pl.ds(row_n, drows), :], lx.at[1])
+    own_h.start()
+    own_n.start()
+
+    @pl.loop(0, acc_ref.shape[0] // 16)
+    def _(i):
+        acc_ref[pl.ds(pl.multiple_of(i * 16, 16), 16), :] = jnp.zeros((16, acc_ref.shape[1]), jnp.float32)
+
+    own_h.wait()
+    own_n.wait()
+    far_send.wait_recv()
+    forward = send(x_ref.at[pl.ds(row_f, drows), :], row_f, drows, 3, sib)
+    forward.start()
+    hid_send.wait_recv()
+    near_send.wait_recv()
+    send(x_ref.at[pl.ds(row_o, drows), :], row_o, drows, 3, sib).wait_recv()
+    forward.wait_send()
+    gain = gain_ref[...].astype(jnp.float32)
+
+    @pl.loop(0, x_ref.shape[0] // 16)
+    def _(i):
+        rows = pl.ds(pl.multiple_of(i * 16, 16), 16)
+        wide = x_ref[rows, :].astype(jnp.float32)
+        factor = lax.rsqrt(jnp.mean(wide * wide, axis=-1, keepdims=True) + EPSILON)
+        x_ref[rows, :] = (wide * factor * gain).astype(jnp.bfloat16)
+
+    def multiply(o, tiles, first, land_ref, own_base):
+        def fetch(t, slot):
+            off = pl.multiple_of(t * TILE, 128)
+
+            @pl.when(o == g)
+            def _():
+                pltpu.make_async_copy(
+                    w_ref.at[:, pl.ds(pl.multiple_of(own_base + off, 128), TILE)], wt_ref.at[slot], lt.at[slot]
+                ).start()
+
+            @pl.when(o != g)
+            def _():
+                pltpu.make_async_copy(
+                    land_ref.at[o, :, pl.ds(off, TILE)], wt_ref.at[slot], lt.at[slot]
+                ).start()
+
+        fetch(0, 0)
+
+        @pl.loop(0, tiles)
+        def _(t):
+            slot = t % 2
+
+            @pl.when(t + 1 < tiles)
+            def _():
+                fetch(t + 1, (t + 1) % 2)
+
+            pltpu.make_async_copy(land_ref.at[0, :, pl.ds(0, TILE)], wt_ref.at[slot], lt.at[slot]).wait()
+            cols = pl.ds(pl.multiple_of(first + t * TILE, 128), TILE)
+            acc_ref[:, cols] += jnp.dot(
+                x_ref[:, pl.ds(pl.multiple_of(o * share, 128), share)], wt_ref[slot],
+                preferred_element_type=jnp.float32,
+            )
+
+    def arrive_b(k):
+        for sign in (-1, 1):
+            zz = z + sign * k
+
+            @pl.when((zz >= 0) & (zz < depth))
+            def _():
+                for yy in (0, 1):
+                    o = zz * 2 + yy
+                    copy_b(o, 2, False).wait_recv()
+                    if sign < 0:
+                        along(copy_b, o, False, z < 0, z + 1 < depth)
+                    else:
+                        along(copy_b, o, False, z >= 1, z < 0)
+
+    def multiply_b(low, high):
+        @pl.loop(0, count)
+        def _(o):
+            hop = o // 2 - z
+
+            @pl.when(((hop >= low) & (hop <= high)) | ((-hop >= low) & (-hop <= high)))
+            def _():
+                multiply(o, tiles_b, cols_a, wb_ref, base_b)
+
+    issue = max(1, depth - 2)
+
+    @pl.loop(0, 4 * (depth + 1))
+    def _(e):
+        k = e // 4
+        s = e % 4
+        side = s // 2
+        right = s % 2
+        kk = k - side
+        zz = z + (2 * right - 1) * kk
+        yy = (y + side) % 2
+        o = zz * 2 + yy
+
+        @pl.when((k == issue) & (s == 2))
+        def _():
+            partner = z * 2 + 1 - y
+            copy_b(partner, 2, False).wait_recv()
+            along(copy_b, g, True, z >= 1, z + 1 < depth)
+            along(copy_b, partner, False, z >= 1, z + 1 < depth)
+
+        @pl.when((k == depth - 1) & (s == 2))
+        def _():
+            for hop in range(1, depth - 1):
+                arrive_b(hop)
+
+        @pl.when((k == depth) & (s == 0))
+        def _():
+            multiply_b(0, depth - 2)
+
+        @pl.when((kk >= 0) & (zz >= 0) & (zz < depth) & ((kk > 0) | (right == 0)))
+        def _():
+            @pl.when(o != g)
+            def _():
+                copy_a(o, 2, False).wait_recv()
+
+            @pl.when((side == 0) & (kk > 0))
+            def _():
+                along(copy_a, o, False, (right == 1) & (z >= 1), (right == 0) & (z + 1 < depth))
+                copy_a(o, 2, False).start()
+
+            multiply(o, tiles_a, 0, wa_ref, base)
+
+    arrive_b(depth - 1)
+    multiply_b(depth - 1, depth - 1)
+
+    far_send.wait_send()
+    hid_send.wait_send()
+    near_send.wait_send()
+
+    @pl.loop(0, count)
+    def _(o):
+        zo = o // 2
+        to_left = (zo >= z) & (z >= 1)
+        to_right = (zo <= z) & (z + 1 < depth)
+
+        @pl.when(o % 2 == y)
+        def _():
+            @pl.when(to_left)
+            def _():
+                copy_a(o, 0, False).wait_send()
+
+            @pl.when(to_right)
+            def _():
+                copy_a(o, 1, False).wait_send()
+
+            copy_a(o, 2, False).wait_send()
+
+        @pl.when(to_left)
+        def _():
+            copy_b(o, 0, False).wait_send()
+
+        @pl.when(to_right)
+        def _():
+            copy_b(o, 1, False).wait_send()
+
+    copy_b(g, 2, False).wait_send()
+
+
+def gather_project(hidden, decode_hidden, norm_gain, qkv_weight, reps):
+    count = lax.axis_size("grp")
+    rows = reps * (hidden.shape[1] + 2 * decode_hidden.shape[3])
+    share = qkv_weight.shape[0]
+    width = hidden.shape[2]
+    cols = qkv_weight.shape[1] // reps
+    tiles = cols // TILE
+    cols_b = max(1, tiles // 5) * TILE
+    cols_a = cols - cols_b
+    hbm = pl.BlockSpec(memory_space=pl.ANY)
+    vmem = pl.BlockSpec(memory_space=pltpu.VMEM)
+    dma = pltpu.SemaphoreType.DMA
+    return pl.pallas_call(
+        functools.partial(gather_kernel, count, rows),
+        out_shape=(
+            jax.ShapeDtypeStruct((rows, cols), jnp.float32),
+            jax.ShapeDtypeStruct((count, share, cols_a), jnp.bfloat16),
+            jax.ShapeDtypeStruct((count, share, cols_b), jnp.bfloat16),
+        ),
+        in_specs=[hbm, hbm, vmem, hbm],
+        out_specs=(vmem, hbm, hbm),
+        scratch_shapes=[
+            pltpu.VMEM((rows, width), jnp.bfloat16),
+            pltpu.VMEM((2, share, TILE), jnp.bfloat16),
+            dma((count, 3)), dma((count,)),
+            dma((count, 3)), dma((count,)),
+            dma((4,)), dma((4,)), dma((2,)), dma((2,)),
+        ],
+        compiler_params=pltpu.CompilerParams(
+            collective_id=0, has_side_effects=True, vmem_limit_bytes=56 << 20
+        ),
+        name="gather_project",
+    )(hidden, decode_hidden, norm_gain.reshape(1, width), qkv_weight)[0]
+
+
+def attend_kernel(prompt_rows, block, len_ref, proj_ref, bias_ref, cos_ref, sin_ref, out_ref, q_ref, k_ref, v_ref, m_ref):
+    rows = proj_ref.shape[0]
+    cosine = cos_ref[...]
+    sine = sin_ref[...]
+    factor = HD ** (-0.5) * math.log2(math.e)
+    valid = len_ref[0]
+
+    def part(j):
+        cols = slice(j * HD, (j + 1) * HD)
+        return proj_ref[:, cols] + bias_ref[:, cols]
+
+    def turned(x):
+        return x * cosine + pltpu.roll(x, HD // 2, 1) * sine
+
+    for j in range(QPK):
+        q_ref[j] = (turned(part(j)) * factor).astype(jnp.bfloat16)
+    k_ref[...] = turned(part(QPK)).astype(jnp.bfloat16)
+    v_ref[...] = part(QPK + 1).astype(jnp.bfloat16)
+
+    def run(start, size, keys):
+        shape = (size, keys)
+        row = lax.broadcasted_iota(jnp.int32, shape, 0) + start
+        col = lax.broadcasted_iota(jnp.int32, shape, 1)
+        if start < prompt_rows:
+            allowed = (col <= row) & (col < valid)
+        else:
+            same = ((row - prompt_rows) // STEPS == (col - prompt_rows) // STEPS) & (col <= row)
+            allowed = (col < jnp.minimum(valid, prompt_rows)) | ((col >= prompt_rows) & same)
+        m_ref[:size, :keys] = jnp.where(allowed, 0.0, NEGATIVE)
+
+        for j in range(QPK):
+            s = lax.dot_general(
+                q_ref[j, start:start + size, :], k_ref[:keys, :], (((1,), (1,)), ((), ())),
+                preferred_element_type=jnp.float32,
+            ) + m_ref[:size, :keys]
+            top = jnp.max(s, axis=-1, keepdims=True)
+            p = jnp.exp2(s - top)
+            total = jnp.sum(p, axis=-1, keepdims=True)
+            o = jnp.dot(p.astype(jnp.bfloat16), v_ref[:keys, :], preferred_element_type=jnp.float32)
+            out_ref[start:start + size, j * HD:(j + 1) * HD] = (o / total).astype(jnp.bfloat16)
+
+    for start in range(0, prompt_rows, block):
+        run(start, block, start + block)
+    run(prompt_rows, rows - prompt_rows, rows)
+
+
+def attend(proj, bias_row, cosine, sine, valid, prompt_rows):
+    rows, cols = proj.shape
+    head = (QPK + 2) * HD
+    heads = cols // head
+    block = 256 if prompt_rows % 256 == 0 else prompt_rows
+    size = max(block, rows - prompt_rows)
+    return pl.pallas_call(
+        functools.partial(attend_kernel, prompt_rows, block),
+        out_shape=jax.ShapeDtypeStruct((rows, heads * QPK * HD), jnp.bfloat16),
+        grid=(heads,),
+        in_specs=[
+            pl.BlockSpec(memory_space=pltpu.SMEM),
+            pl.BlockSpec((rows, head), lambda h: (0, h)),
+            pl.BlockSpec((1, head), lambda h: (0, h)),
+            pl.BlockSpec((rows, HD), lambda h: (0, 0)),
+            pl.BlockSpec((rows, HD), lambda h: (0, 0)),
+        ],
+        out_specs=pl.BlockSpec((rows, QPK * HD), lambda h: (0, h)),
+        scratch_shapes=[
+            pltpu.VMEM((QPK, rows, HD), jnp.bfloat16),
+            pltpu.VMEM((rows, HD), jnp.bfloat16),
+            pltpu.VMEM((rows, HD), jnp.bfloat16),
+            pltpu.VMEM((size, rows), jnp.float32),
+        ],
+        compiler_params=pltpu.CompilerParams(vmem_limit_bytes=48 << 20),
+        name="attend",
+    )(valid.reshape(1), proj, bias_row, cosine, sine)
+
+
+def on_device(hidden, decode_hidden, norm_gain, qkv_weight, qkv_bias, lengths):
+    count = lax.axis_size("grp")
+    reps = lax.axis_size("rep")
+    head_block = (QPK + 2) * HD
+    heads_here = qkv_bias.shape[0] // head_block
+    cols = qkv_weight.shape[1] // reps
+    if reps != 2 or count % 2 or count < 4 or heads_here % reps or cols % TILE or cols < 2 * TILE:
+        return plain_device(hidden, decode_hidden, norm_gain, qkv_weight, qkv_bias, lengths)
+    g = lax.axis_index("grp")
+    r = lax.axis_index("rep")
+    half = count // 2
+    span = hidden.shape[1]
+    drows = decode_hidden.shape[3]
+    prompt_rows = reps * span
+    proj = gather_project(hidden, decode_hidden, norm_gain, qkv_weight, reps)
+
+    index_table = jnp.arange(count, dtype=jnp.int32)
+    own_len = jnp.sum(jnp.where(index_table == g, lengths, 0))
+    steps = jnp.arange(2 * reps * drows, dtype=jnp.int32) % STEPS
+    positions = jnp.concatenate([jnp.arange(prompt_rows, dtype=jnp.int32), own_len + steps])
+    cosine, sine = rope_tables(positions, HD)
+    cosine = jnp.concatenate([cosine, cosine], axis=-1)
+    sine = jnp.concatenate([-sine, sine], axis=-1)
+    bias_row = lax.dynamic_slice_in_dim(qkv_bias, r * cols, cols, 0).astype(jnp.float32).reshape(1, cols)
+    out = attend(proj, bias_row, cosine, sine, own_len, prompt_rows)
+    width = out.shape[1]
+
+    def pick(block, which):
+        return lax.dynamic_index_in_dim(block, which, 0, keepdims=False)
+
+    swap = [(0, 1), (1, 0)]
+    main = out[:prompt_rows].reshape(reps, span, width)
+    near = out[prompt_rows:prompt_rows + 2 * drows].reshape(reps, drows, width)
+    far = out[prompt_rows + 2 * drows:].reshape(reps, drows, width)
+    other_main = lax.ppermute(pick(main, 1 - r), "rep", swap)
+    other_near = lax.ppermute(pick(near, 1 - r), "rep", swap)
+    far_same = lax.ppermute(pick(far, r), "grp", [(p, (p - half) % count) for p in range(count)])
+    cross = [
+        (p * reps + c, ((p - half) % count) * reps + 1 - c) for p in range(count) for c in range(reps)
+    ]
+    far_other = lax.ppermute(pick(far, 1 - r), ("grp", "rep"), cross)
+
+    def join(mine, other):
+        return jnp.where(
+            r == 0, jnp.concatenate([mine, other], axis=-1), jnp.concatenate([other, mine], axis=-1)
+        )
+
+    prefill_out = join(pick(main, r), other_main)[None]
+    decode_out = jnp.stack([join(pick(near, r), other_near), join(far_same, far_other)])[None, None]
+    return (prefill_out, decode_out)
+
+
 def solution(mesh):
     return jax.shard_map(
         on_device,

time: 1130 us -> 507 us (0.45)
  waiting for transfers between devices: 921 us -> 6.11 us
  Pallas kernels: 0 us -> 479 us
  matrix products: 103 us -> 0 us
  local copies, waits for them, and re-layouts: 53.4 us -> 8.03 us
  other arithmetic: 33.8 us -> 8.96 us
  between operations: 14.4 us -> 0.74 us
    all_gather x2 -> x0, waiting for transfers between devices: 893 us -> none  [the longest x1 798 us: on_device(): columns = lax.all_gather(own_cols, 'grp', axis=0, tiled=True)]
    pallas_call x0 -> x2, Pallas kernels: none -> 479 us  [the longest x1 453 us: gather_project(): pl.pallas_call(functools.partial(gather_kernel, count, rows), out_shape=(...]
    dot_general x10 -> x0, matrix products: 76.4 us -> none  [the longest x1 47.5 us: on_device(): projected = jnp.dot(normed, complete, preferred_element_type=jnp.float32)]
    sub x1 -> x0, matrix products: 26.4 us -> none  [on_device(): exponent = jnp.where(allowed, jnp.exp(scores - highest), 0.0)]
    ppermute x2 -> x4, waiting for transfers between devices: 27.4 us -> 6.11 us  [the longest x1 3.38 us: on_device(): lax.ppermute(pick(far, r), 'grp', [(p, (p - half) % count) for p in range...]
    unnamed x32 -> x4, local copies, waits for them, and re-layouts: 22.7 us -> 1.8 us
    convert_element_type x4 -> x0, other arithmetic: 12.4 us -> none  [the longest x2 12.4 us: normalize(): (widened * factor * gain_row.astype(jnp.float32)).astype(jnp.bfloat16)]
  transfers between devices with their start and end apart: 4 -> 4, of which waited for: 3 -> 2; matrix products, arithmetic and copies ran while one was open for 7% -> 1% of each run, Pallas kernels for 0% -> 0%
where the time goes in v1:
time: 507 us; the launch traced here: 506 us
  Pallas kernels  479 us (94%)
  other arithmetic  8.96 us (2%)
  local copies, waits for them, and re-layouts  8.03 us (2%)
  waiting for transfers between devices  6.11 us (1%)
    pallas_call x1, Pallas kernels, gather_project(): pl.pallas_call(functools.partial(gather_kernel, count, rows), out_shape=(...  453 us
    pallas_call x1, Pallas kernels, attend(): pl.pallas_call(functools.partial(attend_kernel, prompt_rows, block), out_...  26.6 us
  transfers between devices with their start and end apart: 4, of which 2 were waited for; matrix products, arithmetic and copies ran while one was open for 1% of the time, Pallas kernels for 0%

profile of v1, /device:TPU:0, one launch (start us, length us, event | category | flops | bytes accessed | tf_op | source)
XLA Modules:
  0.0 506.1 jit_solution(6871452898892023107)
XLA Ops:
  0.7 1.4 reshape.199.gain_ref
  2.0 0.8 dynamic-slice_convert_fusion
  2.8 1.3 fusion.1
  4.1 0.6 fusion.2
  4.8 1.7 fusion
  6.4 0.3 pad_maximum_fusion
  6.8 452.7 %gather_project.1 = (f32[896,2560]{1,0:T(8,128)}, bf16[8,1024,2048]{2,1,0:T(8,128)(2,1)}, bf16[8,1024,512]{2,1,0:T(8,128)(2,1)}) custom-call(bf16[1,384,8192]{2,1,0:T(8,128)(2,1)} %hidden_ref.1, bf16[1,1,2,32,8192]{4,3,2,1,0:T(8,128)(2,1)} %decode_ref.1, bf16[1,8192]{1,0:T(2,128)(2,1)} %reshape.199.gain_ref, bf16[1024,5120]{1,0:T(8,128)(2,1)} %w_ref.1), custom_call_target="tpu_custom_call" | custom-call | tf_op jit(solution)/shard_map/gather_project/pallas_call | solution.py:461
  459.4 26.6 %attend.1 = bf16[896,2048]{1,0:T(8,128)(2,1)S(1)} custom-call(s32[1]{0:T(128)} %bitcast.len_ref, f32[896,2560]{1,0:T(8,128)} %get-tuple-element.3.proj_ref, f32[1,2560]{1,0:T(1,128)S(1)} %reshape.206.bias_ref, f32[896,128]{1,0:T(8,128)S(1)} %get-tuple-element.15.cos_ref, f32[896,128]{1,0:T(8,128)S(1)} %get-tuple-element.16.sin_ref), custom_call_target="tpu_custom_call" | custom-call | tf_op jit(solution)/shard_map/attend/pallas_call | solution.py:536
  486.1 0.0 copy-start
  486.1 1.8 copy-done
  487.9 0.4 slice.12
  488.3 1.9 constant_dynamic-slice_fusion.1
  490.2 0.0 copy-start.1
  490.2 0.0 collective-permute-start
  490.2 1.2 fusion.3
  491.4 0.7 dynamic-slice_bitcast_fusion.2
  492.1 0.0 collective-permute-start.3
  492.1 2.9 collective-permute-start.2
  495.0 0.7 constant_dynamic-slice_fusion
  495.7 0.0 collective-permute-start.1
  495.7 2.7 collective-permute-done.3
  498.4 3.4 collective-permute-done.2
  501.8 0.1 maximum_select_fusion.2
  501.9 0.0 collective-permute-done.1
  501.9 1.0 maximum_select_fusion.1
  503.0 0.8 maximum_bitcast_fusion
  503.8 0.0 collective-permute-done
  503.8 0.0 copy-done.1
  503.8 2.3 maximum_select_fusion
  (4 shorter events, 0.0 us)
Async XLA Ops:
  486.1 1.8 copy-start
  490.2 13.6 %copy-start.1 = (bf16[1,384,2048]{2,1,0:T(8,128)(2,1)S(1)}, bf16[1,384,2048]{2,1,0:T(8,128)(2,1)}, u32[]{:S(2)}) copy-start(bf16[1,384,2048]{2,1,0:T(8,128)(2,1)} %get-tuple-element.6) | copy-start | bytes 4718596
  490.2 13.6 %collective-permute-start = (bf16[384,2048]{1,0:T(8,128)(2,1)}, bf16[384,2048]{1,0:T(8,128)(2,1)S(1)}, u32[]{:S(2)}, u32[]{:S(2)}) collective-permute-start(bf16[384,2048]{1,0:T(8,128)(2,1)} %get-tuple-element.7), channel_id=1, source_target_pairs={{0,2},{2,0},{1,3},{3,1},{4,6},{6,4},{5,7},{7,5},{8,10},{10,8},{9,1... | collective-permute-start | bytes 4718600 | tf_op jit(solution)/shard_map/ppermute | solution.py:593
  492.1 6.3 %collective-permute-start.3 = (bf16[32,2048]{1,0:T(8,128)(2,1)}, bf16[32,2048]{1,0:T(8,128)(2,1)S(1)}, u32[]{:S(2)}, u32[]{:S(2)}) collective-permute-start(bf16[32,2048]{1,0:T(8,128)(2,1)} %get-tuple-element.11), channel_id=1, source_target_pairs={{0,18},{2,16},{4,22},{6,20},{8,26},{10,24},{12,30},{14,28},{16,2},... | collective-permute-start | bytes 393224 | tf_op jit(solution)/shard_map/ppermute | solution.py:599
  492.1 9.7 %collective-permute-start.2 = (bf16[32,2048]{1,0:T(8,128)(2,1)}, bf16[32,2048]{1,0:T(8,128)(2,1)S(1)}, u32[]{:S(2)}, u32[]{:S(2)}) collective-permute-start(bf16[32,2048]{1,0:T(8,128)(2,1)} %get-tuple-element.10), channel_id=1, source_target_pairs={{0,16},{4,20},{8,24},{12,28},{16,0},{20,4},{24,8},{28,12},{1,17},{... | collective-permute-start | bytes 393224 | tf_op jit(solution)/shard_map/ppermute | solution.py:595
  495.7 6.2 %collective-permute-start.1 = (bf16[32,2048]{1,0:T(8,128)(2,1)}, bf16[32,2048]{1,0:T(8,128)(2,1)}, u32[]{:S(2)}, u32[]{:S(2)}) collective-permute-start(bf16[32,2048]{1,0:T(8,128)(2,1)} %get-tuple-element.9), channel_id=1, source_target_pairs={{0,2},{2,0},{1,3},{3,1},{4,6},{6,4},{5,7},{7,5},{8,10},{10,8},{9,1... | collective-permute-start | bytes 393224 | tf_op jit(solution)/shard_map/ppermute | solution.py:594

commit v2 on v1

--- a/solution.py
+++ b/solution.py
@@ -208,7 +208,7 @@
     cols_a = wa_ref.shape[2]
     cols_b = wb_ref.shape[2]
     tiles_a = cols_a // TILE
-    tiles_b = cols_b // TILE
+    rest = cols_a % TILE
     base = pl.multiple_of(r * (cols_a + cols_b), 128)
     base_b = pl.multiple_of(r * (cols_a + cols_b) + cols_a, 128)
 
@@ -312,38 +312,62 @@
         factor = lax.rsqrt(jnp.mean(wide * wide, axis=-1, keepdims=True) + EPSILON)
         x_ref[rows, :] = (wide * factor * gain).astype(jnp.bfloat16)
 
-    def multiply(o, tiles, first, land_ref, own_base):
+    def own_tile(off, n, slot_ref, sem):
+        return pltpu.make_async_copy(w_ref.at[:, pl.ds(pl.multiple_of(base + off, 128), n)], slot_ref, sem)
+
+    def add_product(o, slot, first):
+        cols = pl.ds(pl.multiple_of(first, 128), TILE)
+        acc_ref[:, cols] += jnp.dot(
+            x_ref[:, pl.ds(pl.multiple_of(o * share, 128), share)], wt_ref[slot],
+            preferred_element_type=jnp.float32,
+        )
+
+    def multiply(o):
         def fetch(t, slot):
             off = pl.multiple_of(t * TILE, 128)
 
             @pl.when(o == g)
             def _():
-                pltpu.make_async_copy(
-                    w_ref.at[:, pl.ds(pl.multiple_of(own_base + off, 128), TILE)], wt_ref.at[slot], lt.at[slot]
-                ).start()
+                own_tile(off, TILE, wt_ref.at[slot], lt.at[slot]).start()
 
             @pl.when(o != g)
             def _():
-                pltpu.make_async_copy(
-                    land_ref.at[o, :, pl.ds(off, TILE)], wt_ref.at[slot], lt.at[slot]
-                ).start()
+                pltpu.make_async_copy(wa_ref.at[o, :, pl.ds(off, TILE)], wt_ref.at[slot], lt.at[slot]).start()
 
         fetch(0, 0)
 
-        @pl.loop(0, tiles)
+        @pl.loop(0, tiles_a)
         def _(t):
             slot = t % 2
 
-            @pl.when(t + 1 < tiles)
+            @pl.when(t + 1 < tiles_a)
             def _():
                 fetch(t + 1, (t + 1) % 2)
 
-            pltpu.make_async_copy(land_ref.at[0, :, pl.ds(0, TILE)], wt_ref.at[slot], lt.at[slot]).wait()
-            cols = pl.ds(pl.multiple_of(first + t * TILE, 128), TILE)
-            acc_ref[:, cols] += jnp.dot(
-                x_ref[:, pl.ds(pl.multiple_of(o * share, 128), share)], wt_ref[slot],
-                preferred_element_type=jnp.float32,
-            )
+            own_tile(0, TILE, wt_ref.at[slot], lt.at[slot]).wait()
+            add_product(o, slot, t * TILE)
+
+    def multiply_last(o):
+        first = tiles_a * TILE
+
+        @pl.when(o == g)
+        def _():
+            own_tile(first, TILE, wt_ref.at[0], lt.at[0]).start()
+            own_tile(first, TILE, wt_ref.at[0], lt.at[0]).wait()
+
+        @pl.when(o != g)
+        def _():
+            pieces = [pltpu.make_async_copy(wb_ref.at[o], wt_ref.at[0, :, pl.ds(rest, cols_b)], lt.at[0])]
+            if rest:
+                pieces.append(pltpu.make_async_copy(
+                    wa_ref.at[o, :, pl.ds(first, rest)], wt_ref.at[0, :, pl.ds(0, rest)], lt.at[1]
+                ))
+            for piece in pieces:
+                piece.start()
+            for piece in pieces:
+                piece.wait()
+
+        add_product(o, 0, first)
 
     def arrive_b(k):
         for sign in (-1, 1):
@@ -366,7 +390,7 @@
 
             @pl.when(((hop >= low) & (hop <= high)) | ((-hop >= low) & (-hop <= high)))
             def _():
-                multiply(o, tiles_b, cols_a, wb_ref, base_b)
+                multiply_last(o)
 
     issue = max(1, depth - 2)
 
@@ -408,7 +432,7 @@
                 along(copy_a, o, False, (right == 1) & (z >= 1), (right == 0) & (z + 1 < depth))
                 copy_a(o, 2, False).start()
 
-            multiply(o, tiles_a, 0, wa_ref, base)
+            multiply(o)
 
     arrive_b(depth - 1)
     multiply_b(depth - 1, depth - 1)
@@ -452,8 +476,7 @@
     share = qkv_weight.shape[0]
     width = hidden.shape[2]
     cols = qkv_weight.shape[1] // reps
-    tiles = cols // TILE
-    cols_b = max(1, tiles // 5) * TILE
+    cols_b = min(TILE, max(1, round(cols * 0.15 / 128)) * 128)
     cols_a = cols - cols_b
     hbm = pl.BlockSpec(memory_space=pl.ANY)
     vmem = pl.BlockSpec(memory_space=pltpu.VMEM)
@@ -556,13 +579,76 @@
     )(valid.reshape(1), proj, bias_row, cosine, sine)
 
 
+def exchange_kernel(count, out_ref, prefill_ref, decode_ref, ss, rs, ls):
+    g = lax.axis_index("grp")
+    r = lax.axis_index("rep")
+    far = (g + count // 2) % count
+    span = prefill_ref.shape[1]
+    drows = decode_ref.shape[3]
+    width = out_ref.shape[1]
+    cols = pl.ds(pl.multiple_of(r * width, 128), width)
+    barrier = pltpu.get_barrier_semaphore()
+    for grp, rep in ((g, 1 - r), (far, r), (far, 1 - r)):
+        pl.semaphore_signal(barrier, inc=1, device_id={"grp": grp, "rep": rep}, device_id_type=MESH)
+    pl.semaphore_wait(barrier, 3)
+
+    def rows(start, n):
+        return out_ref.at[pl.ds(pl.multiple_of(start, 16), n), :]
+
+    main = prefill_ref.at[0, :, cols]
+    near = decode_ref.at[0, 0, 0, :, cols]
+    away = decode_ref.at[0, 0, 1, :, cols]
+    near_row = 2 * span
+    far_row = near_row + 2 * drows
+
+    def send(src, dst, i, grp, rep):
+        return pltpu.make_async_remote_copy(
+            src, dst, ss.at[i], rs.at[i], device_id={"grp": grp, "rep": rep}, device_id_type=MESH
+        )
+
+    sends = [
+        send(rows(far_row + r * drows, drows), away, 0, far, r),
+        send(rows(far_row + (1 - r) * drows, drows), away, 1, far, 1 - r),
+        send(rows((1 - r) * span, span), main, 2, g, 1 - r),
+        send(rows(near_row + (1 - r) * drows, drows), near, 3, g, 1 - r),
+    ]
+    local = [
+        pltpu.make_async_copy(rows(r * span, span), main, ls.at[0]),
+        pltpu.make_async_copy(rows(near_row + r * drows, drows), near, ls.at[1]),
+    ]
+    for copy in sends + local:
+        copy.start()
+    for copy in sends + local:
+        copy.wait()
+
+
+def exchange(out, hidden, decode_hidden, reps):
+    dma = pltpu.SemaphoreType.DMA
+    hbm = pl.BlockSpec(memory_space=pl.ANY)
+    width = reps * out.shape[1]
+    return pl.pallas_call(
+        functools.partial(exchange_kernel, lax.axis_size("grp")),
+        out_shape=(
+            jax.ShapeDtypeStruct(hidden.shape[:2] + (width,), jnp.bfloat16),
+            jax.ShapeDtypeStruct(decode_hidden.shape[:4] + (width,), jnp.bfloat16),
+        ),
+        in_specs=[pl.BlockSpec(memory_space=pltpu.VMEM)],
+        out_specs=(hbm, hbm),
+        scratch_shapes=[dma((4,)), dma((4,)), dma((2,))],
+        compiler_params=pltpu.CompilerParams(
+            collective_id=1, has_side_effects=True, vmem_limit_bytes=16 << 20
+        ),
+        name="exchange",
+    )(out)
+
+
 def on_device(hidden, decode_hidden, norm_gain, qkv_weight, qkv_bias, lengths):
     count = lax.axis_size("grp")
     reps = lax.axis_size("rep")
     head_block = (QPK + 2) * HD
     heads_here = qkv_bias.shape[0] // head_block
     cols = qkv_weight.shape[1] // reps
-    if reps != 2 or count % 2 or count < 4 or heads_here % reps or cols % TILE or cols < 2 * TILE:
+    if reps != 2 or count % 2 or count < 4 or heads_here % reps or cols % TILE or cols < 2 * TILE or decode_hidden.shape[1] != 1:
         return plain_device(hidden, decode_hidden, norm_gain, qkv_weight, qkv_bias, lengths)
     g = lax.axis_index("grp")
     r = lax.axis_index("rep")
@@ -581,31 +667,7 @@
     sine = jnp.concatenate([-sine, sine], axis=-1)
     bias_row = lax.dynamic_slice_in_dim(qkv_bias, r * cols, cols, 0).astype(jnp.float32).reshape(1, cols)
     out = attend(proj, bias_row, cosine, sine, own_len, prompt_rows)
-    width = out.shape[1]
-
-    def pick(block, which):
-        return lax.dynamic_index_in_dim(block, which, 0, keepdims=False)
-
-    swap = [(0, 1), (1, 0)]
-    main = out[:prompt_rows].reshape(reps, span, width)
-    near = out[prompt_rows:prompt_rows + 2 * drows].reshape(reps, drows, width)
-    far = out[prompt_rows + 2 * drows:].reshape(reps, drows, width)
-    other_main = lax.ppermute(pick(main, 1 - r), "rep", swap)
-    other_near = lax.ppermute(pick(near, 1 - r), "rep", swap)
-    far_same = lax.ppermute(pick(far, r), "grp", [(p, (p - half) % count) for p in range(count)])
-    cross = [
-        (p * reps + c, ((p - half) % count) * reps + 1 - c) for p in range(count) for c in range(reps)
-    ]
-    far_other = lax.ppermute(pick(far, 1 - r), ("grp", "rep"), cross)
-
-    def join(mine, other):
-        return jnp.where(
-            r == 0, jnp.concatenate([mine, other], axis=-1), jnp.concatenate([other, mine], axis=-1)
-        )
-
-    prefill_out = join(pick(main, r), other_main)[None]
-    decode_out = jnp.stack([join(pick(near, r), other_near), join(far_same, far_other)])[None, None]
-    return (prefill_out, decode_out)
+    return exchange(out, hidden, decode_hidden, reps)
 
 
 def solution(mesh):

time: 507 us -> 488 us (0.963)
  waiting for transfers between devices: 6.11 us -> 0 us
    pallas_call x1, Pallas kernels: 453 us -> 438 us  [gather_project(): pl.pallas_call(functools.partial(gather_kernel, count, rows), out_shape=(...]
    pallas_call x0 -> x1, Pallas kernels: none -> 14.2 us  [exchange(): pl.pallas_call(functools.partial(exchange_kernel, lax.axis_size('grp')),...]
    ppermute x4 -> x0, waiting for transfers between devices: 6.11 us -> none  [the longest x1 3.38 us: on_device(): lax.ppermute(pick(far, r), 'grp', [(p, (p - half) % count) for p in range...]
  transfers between devices with their start and end apart: 4 -> 0, of which waited for: 2 -> 0; matrix products, arithmetic and copies ran while one was open for 1% -> 0% of each run, Pallas kernels for 0% -> 0%
where the time goes in v2:
time: 488 us; the launch traced here: 487 us
  Pallas kernels  479 us (98%)
    pallas_call x1, Pallas kernels, gather_project(): pl.pallas_call(functools.partial(gather_kernel, count, rows), out_shape=(...  438 us
    pallas_call x1, Pallas kernels, attend(): pl.pallas_call(functools.partial(attend_kernel, prompt_rows, block), out_...  26.6 us
    pallas_call x1, Pallas kernels, exchange(): pl.pallas_call(functools.partial(exchange_kernel, lax.axis_size('grp')),...  14.2 us

profile of v2, /device:TPU:0, one launch (start us, length us, event | category | flops | bytes accessed | tf_op | source)
XLA Modules:
  0.0 487.2 jit_solution(18353090482075805535)
XLA Ops:
  0.6 1.3 fusion.1
  1.9 1.3 reshape.33.gain_ref
  3.3 0.0 copy-start
  3.3 437.7 %gather_project.1 = (f32[896,2560]{1,0:T(8,128)}, bf16[8,1024,2176]{2,1,0:T(8,128)(2,1)}, bf16[8,1024,384]{2,1,0:T(8,128)(2,1)}) custom-call(bf16[1,384,8192]{2,1,0:T(8,128)(2,1)} %hidden_ref.1, bf16[1,1,2,32,8192]{4,3,2,1,0:T(8,128)(2,1)} %decode_ref.1, bf16[1,8192]{1,0:T(2,128)(2,1)} %reshape.33.gain_ref, bf16[1024,5120]{1,0:T(8,128)(2,1)} %w_ref.1), custom_call_target="tpu_custom_call" | custom-call | tf_op jit(solution)/shard_map/gather_project/pallas_call | solution.py:484
  441.0 0.0 copy-done
  441.0 0.1 dynamic-slice_convert_fusion
  441.1 0.7 fusion.2
  441.8 1.7 fusion
  443.5 0.3 pad_maximum_fusion
  443.8 26.6 %attend.1.out_ref = bf16[896,2048]{1,0:T(8,128)(2,1)S(1)} custom-call(s32[1]{0:T(128)} %bitcast.len_ref, f32[896,2560]{1,0:T(8,128)} %get-tuple-element.3.proj_ref, f32[1,2560]{1,0:T(1,128)S(1)} %reshape.37.bias_ref, f32[896,128]{1,0:T(8,128)S(1)} %get-tuple-element.7.cos_ref, f32[896,128]{1,0:T(8,128)S(1)} %get-tuple-element.8.sin_ref), custom_call_target="tpu_custom_call" | custom-call | tf_op jit(solution)/shard_map/attend/pallas_call | solution.py:559
  470.5 14.2 %exchange.1 = (bf16[1,384,4096]{2,1,0:T(8,128)(2,1)S(1)}, bf16[1,1,2,32,4096]{4,3,2,1,0:T(8,128)(2,1)S(1)}) custom-call(bf16[896,2048]{1,0:T(8,128)(2,1)S(1)} %attend.1.out_ref), custom_call_target="tpu_custom_call" | custom-call | tf_op jit(solution)/shard_map/exchange/pallas_call | solution.py:629
  484.7 1.7 copy.10
  486.4 0.8 copy.11
  (4 shorter events, 0.0 us)
Async XLA Ops:
  3.3 437.7 %copy-start = (bf16[5120]{0:T(1024)(128)(2,1)S(1)}, bf16[5120]{0:T(1024)(128)(2,1)}, u32[]{:S(2)}) copy-start(bf16[5120]{0:T(1024)(128)(2,1)} %param.10) | copy-start | bytes 30724

commit v3 on v2

--- a/solution.py
+++ b/solution.py
@@ -504,8 +504,54 @@
     )(hidden, decode_hidden, norm_gain.reshape(1, width), qkv_weight)[0]
 
 
-def attend_kernel(prompt_rows, block, len_ref, proj_ref, bias_ref, cos_ref, sin_ref, out_ref, q_ref, k_ref, v_ref, m_ref):
+def attend_kernel(
+    count, heads, block, len_ref, proj_ref, bias_ref, cos_ref, sin_ref, prefill_ref, decode_ref,
+    q_ref, k_ref, v_ref, m_ref, out_ref, ss, rs, ls,
+):
     rows = proj_ref.shape[0]
+    h = pl.program_id(0)
+    g = lax.axis_index("grp")
+    r = lax.axis_index("rep")
+    far = (g + count // 2) % count
+    span = prefill_ref.shape[1]
+    drows = decode_ref.shape[3]
+    prompt_rows = rows - 4 * drows
+    width = QPK * HD
+    barrier = pltpu.get_barrier_semaphore()
+
+    @pl.when(h == 0)
+    def _():
+        for grp, rep in ((g, 1 - r), (far, r), (far, 1 - r)):
+            pl.semaphore_signal(barrier, inc=1, device_id={"grp": grp, "rep": rep}, device_id_type=MESH)
+
+    def copies(i):
+        cols = pl.ds(pl.multiple_of((r * heads + i) * width, 128), width)
+        main = prefill_ref.at[0, :, cols]
+        near = decode_ref.at[0, 0, 0, :, cols]
+        away = decode_ref.at[0, 0, 1, :, cols]
+        near_row = prompt_rows
+        far_row = near_row + 2 * drows
+
+        def piece(start, n):
+            return out_ref.at[i, pl.ds(pl.multiple_of(start, 16), n), :]
+
+        def send(src, dst, c, grp, rep):
+            return pltpu.make_async_remote_copy(
+                src, dst, ss.at[i, c], rs.at[i, c], device_id={"grp": grp, "rep": rep}, device_id_type=MESH
+            )
+
+        first = [
+            send(piece(far_row + r * drows, drows), away, 0, far, r),
+            send(piece(far_row + (1 - r) * drows, drows), away, 1, far, 1 - r),
+            send(piece(near_row + (1 - r) * drows, drows), near, 3, g, 1 - r),
+            pltpu.make_async_copy(piece(near_row + r * drows, drows), near, ls.at[i, 1]),
+        ]
+        second = [
+            send(piece((1 - r) * span, span), main, 2, g, 1 - r),
+            pltpu.make_async_copy(piece(r * span, span), main, ls.at[i, 0]),
+        ]
+        return first, second
+
     cosine = cos_ref[...]
     sine = sin_ref[...]
     factor = HD ** (-0.5) * math.log2(math.e)
@@ -543,22 +589,47 @@
             p = jnp.exp2(s - top)
             total = jnp.sum(p, axis=-1, keepdims=True)
             o = jnp.dot(p.astype(jnp.bfloat16), v_ref[:keys, :], preferred_element_type=jnp.float32)
-            out_ref[start:start + size, j * HD:(j + 1) * HD] = (o / total).astype(jnp.bfloat16)
-
-    for start in range(0, prompt_rows, block):
+            out_ref[h, start:start + size, j * HD:(j + 1) * HD] = (o / total).astype(jnp.bfloat16)
+
+    run(prompt_rows, rows - prompt_rows, rows)
+    run(0, block, block)
+
+    @pl.when(h == 0)
+    def _():
+        pl.semaphore_wait(barrier, 3)
+
+    first, second = copies(h)
+    for copy in first:
+        copy.start()
+    for start in range(block, prompt_rows, block):
         run(start, block, start + block)
-    run(prompt_rows, rows - prompt_rows, rows)
-
-
-def attend(proj, bias_row, cosine, sine, valid, prompt_rows):
+    for copy in second:
+        copy.start()
+
+    @pl.when(h == heads - 1)
+    def _():
+        for i in range(heads):
+            for part_copies in copies(i):
+                for copy in part_copies:
+                    copy.wait()
+
+
+def attend(proj, bias_row, cosine, sine, valid, hidden, decode_hidden, reps):
     rows, cols = proj.shape
     head = (QPK + 2) * HD
     heads = cols // head
+    prompt_rows = reps * hidden.shape[1]
     block = 256 if prompt_rows % 256 == 0 else prompt_rows
     size = max(block, rows - prompt_rows)
+    width = reps * heads * QPK * HD
+    dma = pltpu.SemaphoreType.DMA
+    hbm = pl.BlockSpec(memory_space=pl.ANY)
     return pl.pallas_call(
-        functools.partial(attend_kernel, prompt_rows, block),
-        out_shape=jax.ShapeDtypeStruct((rows, heads * QPK * HD), jnp.bfloat16),
+        functools.partial(attend_kernel, lax.axis_size("grp"), heads, block),
+        out_shape=(
+            jax.ShapeDtypeStruct(hidden.shape[:2] + (width,), jnp.bfloat16),
+            jax.ShapeDtypeStruct(decode_hidden.shape[:4] + (width,), jnp.bfloat16),
+        ),
         grid=(heads,),
         in_specs=[
             pl.BlockSpec(memory_space=pltpu.SMEM),
@@ -567,79 +638,20 @@
             pl.BlockSpec((rows, HD), lambda h: (0, 0)),
             pl.BlockSpec((rows, HD), lambda h: (0, 0)),
         ],
-        out_specs=pl.BlockSpec((rows, QPK * HD), lambda h: (0, h)),
+        out_specs=(hbm, hbm),
         scratch_shapes=[
             pltpu.VMEM((QPK, rows, HD), jnp.bfloat16),
             pltpu.VMEM((rows, HD), jnp.bfloat16),
             pltpu.VMEM((rows, HD), jnp.bfloat16),
             pltpu.VMEM((size, rows), jnp.float32),
+            pltpu.VMEM((heads, rows, QPK * HD), jnp.bfloat16),
+            dma((heads, 4)), dma((heads, 4)), dma((heads, 2)),
         ],
-        compiler_params=pltpu.CompilerParams(vmem_limit_bytes=48 << 20),
+        compiler_params=pltpu.CompilerParams(
+            collective_id=1, has_side_effects=True, vmem_limit_bytes=48 << 20
+        ),
         name="attend",
     )(valid.reshape(1), proj, bias_row, cosine, sine)
-
-
-def exchange_kernel(count, out_ref, prefill_ref, decode_ref, ss, rs, ls):
-    g = lax.axis_index("grp")
-    r = lax.axis_index("rep")
-    far = (g + count // 2) % count
-    span = prefill_ref.shape[1]
-    drows = decode_ref.shape[3]
-    width = out_ref.shape[1]
-    cols = pl.ds(pl.multiple_of(r * width, 128), width)
-    barrier = pltpu.get_barrier_semaphore()
-    for grp, rep in ((g, 1 - r), (far, r), (far, 1 - r)):
-        pl.semaphore_signal(barrier, inc=1, device_id={"grp": grp, "rep": rep}, device_id_type=MESH)
-    pl.semaphore_wait(barrier, 3)
-
-    def rows(start, n):
-        return out_ref.at[pl.ds(pl.multiple_of(start, 16), n), :]
-
-    main = prefill_ref.at[0, :, cols]
-    near = decode_ref.at[0, 0, 0, :, cols]
-    away = decode_ref.at[0, 0, 1, :, cols]
-    near_row = 2 * span
-    far_row = near_row + 2 * drows
-
-    def send(src, dst, i, grp, rep):
-        return pltpu.make_async_remote_copy(
-            src, dst, ss.at[i], rs.at[i], device_id={"grp": grp, "rep": rep}, device_id_type=MESH
-        )
-
-    sends = [
-        send(rows(far_row + r * drows, drows), away, 0, far, r),
-        send(rows(far_row + (1 - r) * drows, drows), away, 1, far, 1 - r),
-        send(rows((1 - r) * span, span), main, 2, g, 1 - r),
-        send(rows(near_row + (1 - r) * drows, drows), near, 3, g, 1 - r),
-    ]
-    local = [
-        pltpu.make_async_copy(rows(r * span, span), main, ls.at[0]),
-        pltpu.make_async_copy(rows(near_row + r * drows, drows), near, ls.at[1]),
-    ]
-    for copy in sends + local:
-        copy.start()
-    for copy in sends + local:
-        copy.wait()
-
-
-def exchange(out, hidden, decode_hidden, reps):
-    dma = pltpu.SemaphoreType.DMA
-    hbm = pl.BlockSpec(memory_space=pl.ANY)
-    width = reps * out.shape[1]
-    return pl.pallas_call(
-        functools.partial(exchange_kernel, lax.axis_size("grp")),
-        out_shape=(
-            jax.ShapeDtypeStruct(hidden.shape[:2] + (width,), jnp.bfloat16),
-            jax.ShapeDtypeStruct(decode_hidden.shape[:4] + (width,), jnp.bfloat16),
-        ),
-        in_specs=[pl.BlockSpec(memory_space=pltpu.VMEM)],
-        out_specs=(hbm, hbm),
-        scratch_shapes=[dma((4,)), dma((4,)), dma((2,))],
-        compiler_params=pltpu.CompilerParams(
-            collective_id=1, has_side_effects=True, vmem_limit_bytes=16 << 20
-        ),
-        name="exchange",
-    )(out)
 
 
 def on_device(hidden, decode_hidden, norm_gain, qkv_weight, qkv_bias, lengths):
@@ -666,8 +678,7 @@
     cosine = jnp.concatenate([cosine, cosine], axis=-1)
     sine = jnp.concatenate([-sine, sine], axis=-1)
     bias_row = lax.dynamic_slice_in_dim(qkv_bias, r * cols, cols, 0).astype(jnp.float32).reshape(1, cols)
-    out = attend(proj, bias_row, cosine, sine, own_len, prompt_rows)
-    return exchange(out, hidden, decode_hidden, reps)
+    return attend(proj, bias_row, cosine, sine, own_len, hidden, decode_hidden, reps)
 
 
 def solution(mesh):

time: 488 us -> 477 us (0.977)
  Pallas kernels: 479 us -> 467 us
    pallas_call x2 -> x1, Pallas kernels: 40.9 us -> 29 us  [attend(): pl.pallas_call(functools.partial(attend_kernel, lax.axis_size('grp'), hea...]
where the time goes in v3:
time: 477 us; the launch traced here: 475 us
  Pallas kernels  467 us (98%)
    pallas_call x1, Pallas kernels, gather_project(): pl.pallas_call(functools.partial(gather_kernel, count, rows), out_shape=(...  438 us
    pallas_call x1, Pallas kernels, attend(): pl.pallas_call(functools.partial(attend_kernel, lax.axis_size('grp'), hea...  29 us

profile of v3, /device:TPU:0, one launch (start us, length us, event | category | flops | bytes accessed | tf_op | source)
XLA Modules:
  0.0 475.2 jit_solution(91506515077233521)
XLA Ops:
  0.6 1.3 fusion.1
  1.9 1.3 reshape.33.gain_ref
  3.3 0.0 copy-start
  3.3 437.7 %gather_project.1 = (f32[896,2560]{1,0:T(8,128)}, bf16[8,1024,2176]{2,1,0:T(8,128)(2,1)}, bf16[8,1024,384]{2,1,0:T(8,128)(2,1)}) custom-call(bf16[1,384,8192]{2,1,0:T(8,128)(2,1)} %hidden_ref.1, bf16[1,1,2,32,8192]{4,3,2,1,0:T(8,128)(2,1)} %decode_ref.1, bf16[1,8192]{1,0:T(2,128)(2,1)} %reshape.33.gain_ref, bf16[1024,5120]{1,0:T(8,128)(2,1)} %w_ref.1), custom_call_target="tpu_custom_call" | custom-call | tf_op jit(solution)/shard_map/gather_project/pallas_call | solution.py:484
  441.0 0.0 copy-done
  441.0 0.1 dynamic-slice_convert_fusion
  441.1 0.7 fusion.2
  441.8 1.7 fusion
  443.5 0.3 pad_maximum_fusion
  443.8 29.0 %attend.1 = (bf16[1,384,4096]{2,1,0:T(8,128)(2,1)S(1)}, bf16[1,1,2,32,4096]{4,3,2,1,0:T(8,128)(2,1)S(1)}) custom-call(s32[1]{0:T(128)} %bitcast.len_ref, f32[896,2560]{1,0:T(8,128)} %get-tuple-element.3.proj_ref, f32[1,2560]{1,0:T(1,128)S(1)} %reshape.37.bias_ref, f32[896,128]{1,0:T(8,128)S(1)} %get-tuple-element.7.cos_ref, ...), custom_call_target="tpu_custom_call" | custom-call | tf_op jit(solution)/shard_map/attend/pallas_call | solution.py:627
  472.8 1.7 copy.10
  474.4 0.8 copy.11
  (4 shorter events, 0.0 us)
Async XLA Ops:
  3.3 437.7 %copy-start = (bf16[5120]{0:T(1024)(128)(2,1)S(1)}, bf16[5120]{0:T(1024)(128)(2,1)}, u32[]{:S(2)}) copy-start(bf16[5120]{0:T(1024)(128)(2,1)} %param.10) | copy-start | bytes 30724
